TPU v7x, 32 devices: a whole 2x2x4 slice. The times are simulated.
32 devices in a mesh: row: 8 (over z, x), col: 4 (over y, core).
Axes of the slice: x: 2, y: 2, z: 4, core: 2. Of those that a mesh axis runs over, the one named last changes fastest.
Arguments:
- panel: float32 [2560, 256], P('row', 'col'), may hold values from 0 to 65520, as said below
- trail: float32 [2560, 16384], P('row', 'col'), may hold values from 0 to 65520, as said below
- leaf_pick: int32 [8, 256], P('row'), may hold values from 0 to 319, as said below
- node_pick: int32 [7, 256], replicated, may hold values from 0 to 511, as said below
Outputs:
- schur: float32 [2560, 16384], P('row', 'col')
- multipliers: float32 [2560, 256], P('row')
Inputs may be any that keep to these rules, and one draw needn't show every extreme that they name: `leaf_pick`: each row holds 256 different local row numbers. `node_pick`: each row holds 256 different positions among the node's 2 * 256 candidates. Entries are whole residues; the panel rows of pivot_ids, in that order, form a unit upper-triangular matrix modulo 65521. `trail`: entries are whole residues.
All inputs are finite; a program needn't handle non-finite values.
Results may differ from a plain program's by a relative error of at most 0.0003.
Values sent between devices are 32-bit elements; how exact they have to be, the bound alone decides.
No kernel may reach another device: no remote copies, remote signals or barrier semaphores. Data moves between devices by JAX's collectives and lax.ppermute only.
A program may use at most 128 MiB of HBM per device.

v0:
```python
import jax
import jax.numpy as jnp
from jax import lax
from jax.sharding import PartitionSpec as P

MODULUS = 65521.0


def swapped(block, axis, bit):
    count = lax.axis_size(axis)
    route = []
    for low in range(count):
        high = low | 1 << bit
        if high != low and high < count:
            route += [(low, high), (high, low)]
    return lax.ppermute(block, axis, route)


def residue(values):
    return jnp.mod(values, MODULUS)


def limbs(values):
    upper_limb = jnp.floor(values / 256.0)
    lower_limb = values - 256.0 * upper_limb
    return (upper_limb.astype(jnp.bfloat16), lower_limb.astype(jnp.bfloat16))


def modmul(first_factor, second_factor):
    first_upper, first_lower = limbs(first_factor)
    second_upper, second_lower = limbs(second_factor)
    high_part = residue(jnp.dot(first_upper, second_upper, preferred_element_type=jnp.float32))
    cross_one = residue(jnp.dot(first_upper, second_lower, preferred_element_type=jnp.float32))
    cross_two = residue(jnp.dot(first_lower, second_upper, preferred_element_type=jnp.float32))
    low_part = residue(jnp.dot(first_lower, second_lower, preferred_element_type=jnp.float32))
    middle = residue(cross_one + cross_two)
    return residue(residue(15.0 * high_part) + residue(256.0 * middle) + low_part)


def invert_unit(pivot_block):
    width = pivot_block.shape[0]
    identity = jnp.eye(width, dtype=jnp.float32)
    nilpotent = pivot_block - identity
    inverse = residue(identity - nilpotent + MODULUS)
    power = nilpotent
    for section in range((width - 1).bit_length() - 1):
        power = modmul(power, power)
        inverse = modmul(inverse, residue(identity + power))
    return inverse


def merge_candidates(owned, partner, place, height, devices, node_pick):
    upper_half = place >> height & 1
    node_index = devices - (devices >> height) + (place >> height + 1)
    picked = node_pick[node_index]

    def join(mine_part, their_part):
        lower_first = jnp.concatenate([mine_part, their_part], axis=0)
        upper_first = jnp.concatenate([their_part, mine_part], axis=0)
        stacked = jnp.where(upper_half == 0, lower_first, upper_first)
        return stacked[picked]

    return jax.tree.map(join, owned, partner)


def per_device(panel, trail, leaf_pick, node_pick):
    row_count = panel.shape[0]
    part_width = panel.shape[1]
    place = lax.axis_index("row")
    devices = lax.axis_size("row")
    depth_count = devices.bit_length() - 1
    own_picks = leaf_pick[0]
    held = (panel[own_picks], place * row_count + own_picks)
    for height in range(depth_count):
        partner = swapped((held[0], held[1]), "row", height)
        held = merge_candidates(held, partner, place, height, devices, node_pick)
    block_part, row_ids = held
    owned = (row_ids // row_count == place).astype(jnp.float32)[:, None]
    local_rows = row_ids % row_count
    pivot_trail = lax.psum(trail[local_rows] * owned, "row")
    pivot_block = lax.all_gather(block_part, "col", axis=1, tiled=True)
    inverse = invert_unit(pivot_block)
    first_col = lax.axis_index("col") * part_width
    inverse_rows = lax.dynamic_slice_in_dim(inverse, first_col, part_width, 0)
    factors = residue(lax.psum(modmul(panel, inverse_rows), "col"))
    remainder = residue(trail + (MODULUS - modmul(factors, pivot_trail)))
    return (remainder / MODULUS, factors / MODULUS)


def solution(mesh):
    in_specs = (P("row", "col"), P("row", "col"), P("row", None), P())
    out_specs = (P("row", "col"), P("row", None))
    return jax.shard_map(
        per_device, mesh=mesh, in_specs=in_specs, out_specs=out_specs, check_vma=False
    )
```

profile of v0, /device:TPU:0, one launch (start us, length us, event | category | flops | bytes accessed | tf_op | source)
XLA Modules:
  0.0 318.1 jit_solution(15602679436969307907)
XLA Ops:
  7.2 1.0 copy.8
  8.2 0.7 compare_select_fusion.4
  8.9 0.7 gather_fusion
  9.6 3.0 collective-permute-start
  12.7 0.7 broadcast_add_fusion.1
  13.4 0.8 compare_select_fusion.1
  14.2 2.7 collective-permute-done.3
  16.9 1.9 gather_fusion.4
  18.9 1.6 collective-permute-start.4
  20.5 2.0 collective-permute-done.4
  22.5 1.9 gather_fusion.5
  24.5 2.7 collective-permute-start.5
  27.1 1.9 collective-permute-done.5
  29.0 1.9 gather_fusion.6
  31.1 0.7 gather_fusion.1
  31.8 1.6 collective-permute-start.1
  33.4 4.7 %collective-permute-done.1 = f32[256,64]{1,0:T(8,128)S(1)} collective-permute-done((f32[256,64]{1,0:T(8,128)S(1)}, f32[256,64]{1,0:T(8,128)S(1)}, u32[]{:S(2)}, u32[]{:S(2)}) %collective-permute-start.1) | collective-permute-done | bytes 65568 | tf_op jit(solution)/shard_map/ppermute | solution.py:16
  38.2 0.7 gather_fusion.2
  38.9 2.7 collective-permute-start.2
  41.6 8.2 %gather_fusion.7 = f32[256,4096]{1,0:T(8,128)} fusion(f32[320,4096]{1,0:T(8,128)} %param.5, s32[1024]{0:T(1024)S(1)} %pad_clamp_fusion), kind=kCustom, calls=%fused_computation.7 | custom fusion | bytes 8389632 | tf_op jit(solution)/shard_map/gather | solution.py:80
  49.8 0.7 gather_fusion.3
  50.7 6.0 %all-gather = f32[256,256]{0,1:T(8,128)S(1)} all-gather(f32[256,64]{0,1:T(8,128)S(1)} %copy.9), channel_id=2, replica_groups=mesh['row'=8,'col'=4] {'col'}, dimensions={1}, use_global_device_ids=true | all-gather | bytes 327680 | tf_op jit(solution)/shard_map/all_gather | solution.py:81
  57.6 0.9 add_select_fusion.127
  58.5 0.5 convolution_remainder_fusion.59
  59.0 0.5 convolution_remainder_fusion.58
  59.5 0.5 convolution_remainder_fusion.57
  60.7 1.2 add_select_fusion.118
  61.9 0.9 add_select_fusion.110
  62.8 0.4 convolution_remainder_fusion.51
  63.2 0.4 convolution_remainder_fusion.50
  63.7 0.4 convolution_remainder_fusion.49
  64.8 1.1 add_select_fusion.101
  65.9 0.9 add_select_fusion.93
  66.8 0.4 convolution_remainder_fusion.43
  67.2 0.4 convolution_remainder_fusion.42
  67.6 0.4 convolution_remainder_fusion.41
  68.8 1.1 add_select_fusion.84
  69.9 1.1 add_select_fusion.76
  71.0 0.4 convolution_remainder_fusion.35
  71.4 0.4 convolution_remainder_fusion.34
  71.8 0.4 convolution_remainder_fusion.33
  73.0 1.1 add_select_fusion.67
  74.0 0.9 add_select_fusion.59
  75.0 0.4 convolution_remainder_fusion.27
  75.3 0.4 convolution_remainder_fusion.26
  75.8 0.4 convolution_remainder_fusion.25
  76.9 1.1 add_select_fusion.50
  78.0 0.9 add_select_fusion.42
  78.9 0.4 convolution_remainder_fusion.19
  79.3 0.4 convolution_remainder_fusion.18
  79.7 0.4 convolution_remainder_fusion.17
  80.9 1.1 add_select_fusion.33
  82.0 1.1 add_select_fusion.24
  83.0 0.4 add_select_fusion.22
  84.0 1.0 add_select_fusion.18
  86.1 1.9 add_select_fusion.10
  88.0 4.8 %broadcast_multiply_fusion = f32[256,4096]{1,0:T(8,128)} fusion(f32[256,4096]{1,0:T(8,128)} %gather_fusion.7, f32[256]{0:T(256)S(1)} %compare_convert_fusion), kind=kLoop, calls=%fused_computation.37 | loop fusion | flops 1048576 | bytes 8389632 | tf_op jit(solution)/shard_map/mul | solution.py:80
  92.8 25.4 %all-reduce.3.cloned.1.call-done = f32[320,256]{1,0:T(8,128)} async-done(((f32[320,256]{1,0:T(8,128)}), f32[320,256]{1,0:T(8,128)}) %all-reduce.3.cloned.1.call-update) | async-done | bytes 327696 | tf_op jit(solution)/shard_map/psum | solution.py:85
  118.3 1.9 broadcast_multiply_fusion.1
  120.1 158.8 %all-reduce.5.cloned.1.call-done = f32[256,4096]{1,0:T(8,128)} async-done(((f32[256,4096]{1,0:T(8,128)}), f32[256,4096]{1,0:T(8,128)}) %all-reduce.5.cloned.1.call-update) | async-done | bytes 4194320 | tf_op jit(solution)/shard_map/psum | solution.py:80
  279.0 4.5 %convolution_remainder_fusion.3 = f32[320,4096]{1,0:T(8,128)S(1)} fusion(f32[256,4096]{1,0:T(8,128)} %all-reduce.5.cloned.1.call-done, f32[320,256]{1,0:T(8,128)} %all-reduce.3.cloned.1.call-done), kind=kOutput, calls=%fused_computation.20 | convolution fusion | flops 676282368 | bytes 9764864 | tf_op jit(solution)/shard_map/dot_general | solution.py:32
  283.5 2.8 convolution_remainder_fusion.2
  286.3 2.6 convolution_remainder_fusion.1
  288.9 22.2 %fusion.12 = f32[320,4096]{1,0:T(8,128)} fusion(f32[320,4096]{1,0:T(8,128)S(1)} %bitcast.22, f32[320,4096]{1,0:T(8,128)S(1)} %convolution_remainder_fusion.1, f32[320,4096]{1,0:T(8,128)S(1)} %convolution_remainder_fusion.2, f32[320,4096]{1,0:T(8,128)S(1)} %convolution_remainder_fusion.3, f32[256,4096]{1,0:T(8,128)S(1)} %copy-done, f32[320,256]{1,0:T(8,128)S(1)} %copy-done.1), kind=kOutput, calls=%fused_computation.33 | convolution fusion | flops 754565120 | bytes 30736384 | tf_op jit(solution)/shard_map/dot_general | solution.py:35
  (62 shorter events, 7.5 us)
Async XLA Ops:
  7.2 111.1 %all-reduce.3.cloned.1.call-start = ((), (), s32[]{:S(2)}) async-start(), calls=%async_computation | async-start | bytes 655360 | tf_op jit(solution)/shard_map/psum | solution.py:85
  9.6 21.4 %collective-permute-start = (f32[256,64]{1,0:T(8,128)S(1)}, f32[256,64]{1,0:T(8,128)S(1)}, u32[]{:S(2)}, u32[]{:S(2)}) collective-permute-start(f32[256,64]{1,0:T(8,128)S(1)} %gather_fusion), channel_id=1, source_target_pairs={{0,4},{4,0},{8,12},{12,8},{16,20},{20,16},{24,28},{28,24},{1,5},{5... | collective-permute-start | bytes 196616 | tf_op jit(solution)/shard_map/ppermute | solution.py:16
  13.3 3.6 %collective-permute-start.3 = (s32[256]{0:T(256)S(1)}, s32[256]{0:T(256)S(1)}, u32[]{:S(2)}, u32[]{:S(2)}) collective-permute-start(s32[256]{0:T(256)S(1)} %bitcast.29), channel_id=1, source_target_pairs={{0,4},{4,0},{8,12},{12,8},{16,20},{20,16},{24,28},{28,24},{1,5},{5... | collective-permute-start | bytes 3080 | tf_op jit(solution)/shard_map/ppermute | solution.py:16
  18.9 3.6 %collective-permute-start.4 = (s32[256]{0:T(256)S(1)}, s32[256]{0:T(256)S(1)}, u32[]{:S(2)}, u32[]{:S(2)}) collective-permute-start(s32[256]{0:T(256)S(1)} %gather_fusion.4), channel_id=1, source_target_pairs={{0,8},{8,0},{4,12},{12,4},{16,24},{24,16},{20,28},{28,20},{1,9},{9... | collective-permute-start | bytes 3080 | tf_op jit(solution)/shard_map/ppermute | solution.py:16
  24.5 4.5 %collective-permute-start.5 = (s32[256]{0:T(256)S(1)}, s32[256]{0:T(256)S(1)}, u32[]{:S(2)}, u32[]{:S(2)}) collective-permute-start(s32[256]{0:T(256)S(1)} %gather_fusion.5), channel_id=1, source_target_pairs={{0,16},{16,0},{4,20},{20,4},{8,24},{24,8},{12,28},{28,12},{1,17},{... | collective-permute-start | bytes 3080 | tf_op jit(solution)/shard_map/ppermute | solution.py:16
  31.8 6.3 %collective-permute-start.1 = (f32[256,64]{1,0:T(8,128)S(1)}, f32[256,64]{1,0:T(8,128)S(1)}, u32[]{:S(2)}, u32[]{:S(2)}) collective-permute-start(f32[256,64]{1,0:T(8,128)S(1)} %gather_fusion.1), channel_id=1, source_target_pairs={{0,8},{8,0},{4,12},{12,4},{16,24},{24,16},{20,28},{28,20},{1,9},{9... | collective-permute-start | bytes 196616 | tf_op jit(solution)/shard_map/ppermute | solution.py:16
  38.9 10.9 %collective-permute-start.2 = (f32[256,64]{1,0:T(8,128)S(1)}, f32[256,64]{1,0:T(8,128)S(1)}, u32[]{:S(2)}, u32[]{:S(2)}) collective-permute-start(f32[256,64]{1,0:T(8,128)S(1)} %gather_fusion.2), channel_id=1, source_target_pairs={{0,16},{16,0},{4,20},{20,4},{8,24},{24,8},{12,28},{28,12},{1,17},{... | collective-permute-start | bytes 196616 | tf_op jit(solution)/shard_map/ppermute | solution.py:16
  82.0 3.2 copy-start.2
  88.0 191.0 %all-reduce.5.cloned.1.call-start = ((), (), s32[]{:S(2)}) async-start(), calls=%async_computation.1 | async-start | bytes 8388608 | tf_op jit(solution)/shard_map/psum | solution.py:80
  120.1 163.3 %copy-start.1 = (f32[320,256]{1,0:T(8,128)S(1)}, f32[320,256]{1,0:T(8,128)}, u32[]{:S(2)}) copy-start(f32[320,256]{1,0:T(8,128)} %all-reduce.3.cloned.1.call-done) | copy-start | bytes 983044
  279.0 4.5 %copy-start = (f32[256,4096]{1,0:T(8,128)S(1)}, f32[256,4096]{1,0:T(8,128)}, u32[]{:S(2)}) copy-start(f32[256,4096]{1,0:T(8,128)} %all-reduce.5.cloned.1.call-done) | copy-start | bytes 12582916
  283.5 5.4 %slice-start = ((s8[5242880]{0:T(1024)(128)(4,1)}), s8[4194304]{0:T(1024)(128)(4,1)S(1)}, s32[]{:S(2)}) async-start(s8[5242880]{0:T(1024)(128)(4,1)} %bitcast.21), calls=%async_computation.2 | async-start | bytes 8388608
  286.3 2.6 slice-start.1
Sparse Core Ops, SparseCore 0:
  88.1 30.1 all-reduce.2
  122.5 156.3 all-reduce.4
where the time goes:
time: 323 us; the launch traced here: 318 us
  waiting for transfers between devices  196 us (61%)
  matrix products  62.6 us (19%)
  local copies, waits for them, and re-layouts  18.2 us (6%)
  between operations  14.8 us (5%)
  starting transfers between devices  11.8 us (4%)
  other arithmetic  9.13 us (3%)
  blocking collectives  5.95 us (2%)
    psum x1, waiting for transfers between devices, per_device(): pivot_trail = lax.psum(trail[local_rows] * owned, 'row')  159 us
    dot_general x16, matrix products, modmul(): jnp.dot(first_lower, second_lower, preferred_element_type=jnp.float32)  37.5 us
    psum x1, waiting for transfers between devices, per_device(): factors = residue(lax.psum(modmul(panel, inverse_rows), 'col'))  25.4 us
    ppermute x6, starting transfers between devices, swapped(): return lax.ppermute(block, axis, route)  11.7 us
    ppermute x6, waiting for transfers between devices, swapped(): return lax.ppermute(block, axis, route)  11.3 us
    dot_general x16, matrix products, modmul(): jnp.dot(first_upper, second_upper, preferred_element_type=jnp.float32)  9.38 us
    gather x1, local copies, waits for them, and re-layouts, per_device(): pivot_trail = lax.psum(trail[local_rows] * owned, 'row')  8.18 us
    gather x7, local copies, waits for them, and re-layouts, join(): return stacked[picked]  8.1 us
  transfers between devices with their start and end apart: 8, of which 6 were waited for; matrix products, arithmetic and copies ran while one was open for 7% of the time, Pallas kernels for 0%

commit v1 on v0

--- a/solution.py
+++ b/solution.py
@@ -77,7 +77,7 @@
     block_part, row_ids = held
     owned = (row_ids // row_count == place).astype(jnp.float32)[:, None]
     local_rows = row_ids % row_count
-    pivot_trail = lax.psum(trail[local_rows] * owned, "row")
+    pivot_trail = jnp.sum(lax.all_gather(trail[local_rows] * owned, "row"), axis=0)
     pivot_block = lax.all_gather(block_part, "col", axis=1, tiled=True)
     inverse = invert_unit(pivot_block)
     first_col = lax.axis_index("col") * part_width

time: 323 us -> 786 us (2.43)
  waiting for transfers between devices: 196 us -> 640 us
  other arithmetic: 9.13 us -> 23.6 us
    all_gather x0 -> x1, waiting for transfers between devices: none -> 608 us  [per_device(): lax.all_gather(trail[local_rows] * owned, 'row')]
    psum x1 -> x0, waiting for transfers between devices: 159 us -> none  [per_device(): pivot_trail = lax.psum(trail[local_rows] * owned, 'row')]
    reduce_sum x0 -> x1, other arithmetic: none -> 14 us  [per_device(): jnp.sum(lax.all_gather(trail[local_rows] * owned, 'row'), axis=0)]
  transfers between devices with their start and end apart: 8 -> 8, of which waited for: 6 -> 5; matrix products, arithmetic and copies ran while one was open for 7% -> 3% of each run, Pallas kernels for 0% -> 0%
where the time goes in v1:
time: 786 us; the launch traced here: 781 us
  waiting for transfers between devices  640 us (81%)
  matrix products  62.2 us (8%)
  other arithmetic  23.6 us (3%)
  local copies, waits for them, and re-layouts  18.2 us (2%)
  between operations  16.3 us (2%)
  starting transfers between devices  14.2 us (2%)
    all_gather x1, waiting for transfers between devices, per_device(): lax.all_gather(trail[local_rows] * owned, 'row')  608 us
    dot_general x16, matrix products, modmul(): jnp.dot(first_lower, second_lower, preferred_element_type=jnp.float32)  37.3 us
    psum x1, waiting for transfers between devices, per_device(): factors = residue(lax.psum(modmul(panel, inverse_rows), 'col'))  26.2 us
  transfers between devices with their start and end apart: 8, of which 5 were waited for; matrix products, arithmetic and copies ran while one was open for 3% of the time, Pallas kernels for 0%

profile of v1, /device:TPU:0, one launch (start us, length us, event | category | flops | bytes accessed | tf_op | source)
XLA Modules:
  0.0 780.8 jit_solution(15529044774534345553)
XLA Ops:
  8.0 0.7 broadcast_add_fusion.1
  8.7 3.0 collective-permute-start.3
  11.7 0.7 compare_select_fusion.4
  12.4 1.0 copy.8
  13.4 0.7 gather_fusion
  14.2 0.8 compare_select_fusion.1
  15.1 1.9 gather_fusion.4
  17.0 2.1 collective-permute-start.4
  19.2 1.5 collective-permute-done.4
  20.7 1.9 gather_fusion.5
  22.7 3.1 collective-permute-start.5
  25.8 1.5 collective-permute-done.5
  27.4 1.9 gather_fusion.6
  29.4 0.7 gather_fusion.1
  30.1 2.0 collective-permute-start.1
  32.1 3.0 collective-permute-done.1
  35.2 0.7 gather_fusion.2
  35.9 3.8 collective-permute-start.2
  39.8 8.2 %gather_fusion.7 = f32[256,4096]{1,0:T(8,128)} fusion(f32[320,4096]{1,0:T(8,128)} %param.5, s32[1024]{0:T(1024)S(1)} %pad_clamp_fusion), kind=kCustom, calls=%fused_computation.7 | custom fusion | bytes 8389632 | tf_op jit(solution)/shard_map/gather | solution.py:80
  48.0 0.7 gather_fusion.3
  48.8 6.0 all-gather
  55.7 0.9 add_select_fusion.127
  57.4 0.9 add_select_fusion.110
  59.1 0.9 add_select_fusion.93
  60.8 0.9 add_select_fusion.76
  62.5 0.9 add_select_fusion.59
  64.2 0.9 add_select_fusion.42
  65.9 0.5 convolution_remainder_fusion.57
  66.4 0.5 convolution_remainder_fusion.58
  66.9 0.5 convolution_remainder_fusion.59
  67.3 1.2 add_select_fusion.118
  68.5 0.6 convolution_remainder_fusion.49
  69.1 0.4 convolution_remainder_fusion.50
  69.5 0.4 convolution_remainder_fusion.51
  69.9 1.1 add_select_fusion.101
  71.0 0.4 convolution_remainder_fusion.41
  71.4 0.4 convolution_remainder_fusion.42
  71.8 0.4 convolution_remainder_fusion.43
  72.2 1.1 add_select_fusion.84
  73.3 0.4 convolution_remainder_fusion.33
  73.7 0.4 convolution_remainder_fusion.34
  74.1 0.4 convolution_remainder_fusion.35
  74.5 1.1 add_select_fusion.67
  75.9 0.4 convolution_remainder_fusion.26
  76.4 0.4 convolution_remainder_fusion.27
  76.8 1.1 add_select_fusion.50
  77.8 0.4 convolution_remainder_fusion.17
  78.2 0.4 convolution_remainder_fusion.18
  78.6 0.4 convolution_remainder_fusion.19
  79.0 1.1 add_select_fusion.24
  80.1 1.1 add_select_fusion.33
  81.7 0.4 add_select_fusion.22
  82.1 0.5 compare_and_fusion
  82.6 0.6 add_select_fusion.18
  84.2 1.9 add_select_fusion.10
  86.1 4.8 bitcast_multiply_fusion
  91.0 26.2 %all-reduce.2.cloned.1.call-done = f32[320,256]{1,0:T(8,128)} async-done(((f32[320,256]{1,0:T(8,128)}), f32[320,256]{1,0:T(8,128)}) %all-reduce.2.cloned.1.call-update) | async-done | bytes 327696 | tf_op jit(solution)/shard_map/psum | solution.py:85
  117.2 1.9 broadcast_multiply_fusion
  119.0 608.0 %all-gather.3.cloned.1.call-done = f32[8,256,4096]{2,1,0:T(8,128)} async-done(((f32[1,256,4096]{2,1,0:T(8,128)}), f32[8,256,4096]{2,1,0:T(8,128)}) %all-gather.3.cloned.1.call-update) | async-done | bytes 33554448 | tf_op jit(solution)/shard_map/all_gather | solution.py:80
  727.1 14.0 %reduce_sum.9 = f32[256,4096]{1,0:T(8,128)} reduce(f32[8,256,4096]{2,1,0:T(8,128)} %all-gather.3.cloned.1.call-done, f32[]{:T(128)} %constant.375.clone.1), dimensions={0}, to_apply=%region_1.2 | reduce | flops 7340032 | bytes 37748740 | tf_op jit(solution)/shard_map/reduce_sum | solution.py:80
  741.1 4.5 convolution_remainder_fusion.1
  745.6 2.8 convolution_remainder_fusion.2
  748.4 2.5 convolution_remainder_fusion.3
  751.0 22.2 %fusion.12 = f32[320,4096]{1,0:T(8,128)} fusion(f32[320,4096]{1,0:T(8,128)S(1)} %bitcast.24, f32[320,4096]{1,0:T(8,128)S(1)} %convolution_remainder_fusion.1, f32[320,4096]{1,0:T(8,128)S(1)} %convolution_remainder_fusion.2, f32[320,4096]{1,0:T(8,128)S(1)} %convolution_remainder_fusion.3, f32[256,4096]{1,0:T(8,128)S(1)} %copy-done, f32[320,256]{1,0:T(8,128)S(1)} %copy-done.1), kind=kOutput, calls=%fused_computation.33 | convolution fusion | flops 754565120 | bytes 30736384 | tf_op jit(solution)/shard_map/dot_general | solution.py:35
  (63 shorter events, 7.8 us)
Async XLA Ops:
  8.0 109.2 %all-reduce.2.cloned.1.call-start = ((), (), s32[]{:S(2)}) async-start(), calls=%async_computation | async-start | bytes 655360 | tf_op jit(solution)/shard_map/psum | solution.py:85
  8.7 6.3 collective-permute-start.3
  14.1 15.2 %collective-permute-start = (f32[256,64]{1,0:T(8,128)S(1)}, f32[256,64]{1,0:T(8,128)S(1)}, u32[]{:S(2)}, u32[]{:S(2)}) collective-permute-start(f32[256,64]{1,0:T(8,128)S(1)} %gather_fusion), channel_id=1, source_target_pairs={{0,4},{4,0},{8,12},{12,8},{16,20},{20,16},{24,28},{28,24},{1,5},{5... | collective-permute-start | bytes 196616 | tf_op jit(solution)/shard_map/ppermute | solution.py:16
  17.0 3.7 collective-permute-start.4
  22.7 4.7 collective-permute-start.5
  30.1 5.0 collective-permute-start.1
  35.9 12.0 %collective-permute-start.2 = (f32[256,64]{1,0:T(8,128)S(1)}, f32[256,64]{1,0:T(8,128)S(1)}, u32[]{:S(2)}, u32[]{:S(2)}) collective-permute-start(f32[256,64]{1,0:T(8,128)S(1)} %gather_fusion.2), channel_id=1, source_target_pairs={{0,16},{16,0},{4,20},{20,4},{8,24},{24,8},{12,28},{28,12},{1,17},{... | collective-permute-start | bytes 196616 | tf_op jit(solution)/shard_map/ppermute | solution.py:16
  81.2 2.1 copy-start.2
  86.1 641.0 %all-gather.3.cloned.1.call-start = ((), (), s32[]{:S(2)}) async-start(), calls=%async_computation.1 | async-start | bytes 37748736 | tf_op jit(solution)/shard_map/all_gather | solution.py:80
  119.0 622.0 %copy-start.1 = (f32[320,256]{1,0:T(8,128)S(1)}, f32[320,256]{1,0:T(8,128)}, u32[]{:S(2)}) copy-start(f32[320,256]{1,0:T(8,128)} %all-reduce.2.cloned.1.call-done) | copy-start | bytes 983044
  741.1 4.5 copy-start
  745.6 5.4 slice-start
  748.4 2.6 slice-start.1
Sparse Core Ops, SparseCore 0:
  86.2 30.9 all-reduce.1
Sparse Core Ops, SparseCore 1:
  91.0 636.0 all-gather.2
